TPU v7x, 256 devices: a whole 4x4x8 slice. The times are simulated.
256 devices in a mesh: dp: 8 (over y, core), expert: 32 (over z, x).
Axes of the slice: x: 4, y: 4, z: 8, core: 2. Of those that a mesh axis runs over, the one named last changes fastest.
Arguments:
- tokens: bfloat16 [32768, 4096], P(('dp', 'expert')), may hold values from -6 to 6
- out_grad: bfloat16 [32768, 4096], P(('dp', 'expert')), may hold values from -0.29882812 to 0.29882812
- probs: bfloat16 [32768, 8], P(('dp', 'expert')), may hold values from 0.049804688 to 0.5
- routes: int32 [32768, 8], P(('dp', 'expert')), may hold values from 0 to 127, as said below
- saved_gate: bfloat16 [131072, 768], P(('dp', 'expert')), may hold values from -6 to 6
- saved_up: bfloat16 [131072, 768], P(('dp', 'expert')), may hold values from -6 to 6
- down_weight: bfloat16 [32, 768, 4096], P('expert'), may hold values from -0.21875 to 0.21875
Outputs:
- grad_down: float32 [32, 768, 4096], P('expert', 'dp')
- grad_up: bfloat16 [32, 4096, 768], P('expert', 'dp')
- prob_grad: float32 [32768, 8], P(('dp', 'expert'))
Inputs may be any that keep to these rules, and one draw needn't show every extreme that they name: `routes`: each row names 8 different experts. In every aligned block of 128 rows at least half of the rows name one common expert whose number is a multiple of 4; which one is drawn from the seed.
All inputs are finite; a program needn't handle non-finite values.
Results may differ from a plain program's by a relative error of at most 0.014.
Values may be sent and summed in bfloat16 or wider, within the bound.
A program may use at most 192 MiB of HBM per device.

v0:
```python
import jax
import jax.numpy as jnp
from jax import lax
from jax.sharding import PartitionSpec as P

EXP_DEV = 4


def per_device(tokens, out_grad, probs, routes, saved_gate, saved_up, down_weight):
    owners = lax.axis_size("expert")
    groups = lax.axis_size("dp")
    tok_count = tokens.shape[0]
    model_width = tokens.shape[1]
    slot_rows = saved_gate.shape[0]
    capacity = slot_rows // owners
    hidden_width = saved_gate.shape[1]
    in_window = routes % EXP_DEV == 0
    target = routes // EXP_DEV
    owner_ids = jnp.arange(owners, dtype=jnp.int32)
    routed = jnp.sum(
        ((target[:, :, None] == owner_ids[None, None, :]) & in_window[:, :, None]).astype(
            jnp.int32
        ),
        axis=1,
    )
    before = jnp.cumsum(routed, axis=0) - routed
    position = jnp.take_along_axis(before, target, axis=1)
    retained = in_window & (position < capacity)
    slot_index = jnp.where(retained, target * capacity + position, slot_rows)
    flat_index = slot_index.reshape(-1)
    token_ids = jnp.broadcast_to(jnp.arange(tok_count, dtype=jnp.int32)[:, None], routes.shape)
    holders = (
        jnp.full((slot_rows,), -1, jnp.int32).at[flat_index].set(token_ids.reshape(-1), mode="drop")
    )
    weight_slot = (
        jnp.zeros((slot_rows,), jnp.bfloat16).at[flat_index].set(probs.reshape(-1), mode="drop")
    )
    filled = holders >= 0
    safe_rows = jnp.maximum(holders, 0)
    send_x = jnp.where(filled[:, None], tokens[safe_rows], jnp.zeros((), jnp.bfloat16)).reshape(
        owners, capacity, model_width
    )
    send_dy = jnp.where(filled[:, None], out_grad[safe_rows], jnp.zeros((), jnp.bfloat16)).reshape(
        owners, capacity, model_width
    )
    send_weight = weight_slot.reshape(owners, capacity)
    recv_x, recv_dy, recv_weight = (
        lax.all_to_all(send_x, "expert", split_axis=0, concat_axis=0, tiled=True),
        lax.all_to_all(send_dy, "expert", split_axis=0, concat_axis=0, tiled=True),
        lax.all_to_all(send_weight, "expert", split_axis=0, concat_axis=0, tiled=True),
    )
    recv_x = recv_x.reshape(slot_rows, model_width)
    recv_dy = recv_dy.reshape(slot_rows, model_width)
    weights = recv_weight.reshape(slot_rows).astype(jnp.float32)
    gate_act = jax.nn.silu(saved_gate.astype(jnp.float32))
    hidden = (gate_act * saved_up.astype(jnp.float32)).astype(jnp.bfloat16)
    matrix = down_weight[0]
    back_grad = lax.dot_general(
        recv_dy, matrix, (((1,), (1,)), ((), ())), preferred_element_type=jnp.float32
    )
    projected = jnp.dot(hidden, matrix, preferred_element_type=jnp.float32)
    slot_grad = jnp.sum(recv_dy.astype(jnp.float32) * projected, axis=1)
    returned = lax.all_to_all(
        slot_grad.reshape(owners, capacity), "expert", split_axis=0, concat_axis=0, tiled=True
    )
    gathered_grad = returned.reshape(-1)[jnp.minimum(slot_index, slot_rows - 1)]
    prob_grad = jnp.where(retained, gathered_grad, jnp.zeros((), jnp.float32))
    scaled = (weights[:, None] * recv_dy.astype(jnp.float32)).astype(jnp.bfloat16)
    grad_pre = (weights[:, None] * back_grad * gate_act).astype(jnp.bfloat16)
    column_block = hidden
    down_share = lax.psum_scatter(
        lax.dot_general(
            column_block, scaled, (((0,), (0,)), ((), ())), preferred_element_type=jnp.float32
        ),
        "dp",
        scatter_dimension=0,
        tiled=True,
    )
    column_block = recv_x
    product = lax.dot_general(
        column_block, grad_pre, (((0,), (0,)), ((), ())), preferred_element_type=jnp.float32
    )
    up_share = lax.psum_scatter(
        lax.optimization_barrier(product.astype(jnp.bfloat16))
        .astype(jnp.float32)
        .astype(jnp.bfloat16),
        "dp",
        scatter_dimension=0,
        tiled=True,
    )
    return (
        down_share.reshape(1, hidden_width // groups, model_width),
        up_share.reshape(1, model_width // groups, hidden_width),
        prob_grad,
    )


def solution(mesh):
    in_specs = (
        P(("dp", "expert"), None),
        P(("dp", "expert"), None),
        P(("dp", "expert"), None),
        P(("dp", "expert"), None),
        P(("dp", "expert"), None),
        P(("dp", "expert"), None),
        P("expert", None, None),
    )
    out_specs = (P("expert", "dp", None), P("expert", "dp", None), P(("dp", "expert"), None))
    return jax.shard_map(
        per_device, mesh=mesh, in_specs=in_specs, out_specs=out_specs, check_vma=False
    )
```

profile of v0, /device:TPU:1, one launch (start us, length us, event | category | flops | bytes accessed | tf_op | source)
XLA Modules:
  0.0 396.8 jit_solution(17557870057042219985)
XLA Ops:
  7.2 0.9 copy.26
  8.2 0.8 copy.34
  9.6 7.1 %gather_fusion.3 = s32[1024]{0:T(1024)S(1)} fusion(s32[128,32]{1,0:T(8,128)S(1)} %sub.10, s32[1024]{0:T(1024)S(1)} %reshape.135), kind=kCustom, calls=%fused_computation.3 | custom fusion | bytes 16384 | tf_op jit(solution)/shard_map/jit(take_along_axis)/gather | solution.py:27
  17.0 7.6 %scatter_custom_fusion = bf16[512]{0:T(512)(128)(2,1)S(1)} fusion(s32[1024]{0:T(1024)S(1)} %bitcast.29, bf16[1024]{0:T(1024)(128)(2,1)S(1)} %reshape.145, bf16[]{:T(256)} %constant.39.clone.1), kind=kCustom, calls=%fused_computation.52 | custom fusion | bytes 1026 | tf_op jit(solution)/shard_map/scatter | solution.py:36
  24.6 0.7 all_to_all.24
  25.3 11.9 %all-to-all-start = ((bf16[32,1,16]{2,1,0:T(2,128)(2,1)}), bf16[32,1,16]{2,1,0:T(2,128)(2,1)S(1)}, u32[]{:S(2)}, u32[]{:S(2)}) async-start(bf16[32,1,16]{2,1,0:T(2,128)(2,1)} %all_to_all.24), calls=%async_computation | async-start | bytes 32768 | tf_op jit(solution)/shard_map/all_to_all | solution.py:50
  37.2 4.3 %scatter_custom_fusion.1 = s32[512]{0:T(512)S(1)} fusion(s32[1024]{0:T(1024)S(1)} %bitcast.30, s32[1024]{0:T(1024)S(1)} %reshape.153, s32[]{:T(128)} %constant.61.clone.1), kind=kCustom, calls=%fused_computation.50 | custom fusion | bytes 2052 | tf_op jit(solution)/shard_map/scatter | solution.py:33
  41.7 4.4 %gather_fusion.1 = bf16[512,4096]{1,0:T(8,128)(2,1)} fusion(bf16[128,4096]{1,0:T(8,128)(2,1)S(1)} %copy-done, s32[1024]{0:T(1024)S(1)} %pad_clamp_fusion), kind=kCustom, calls=%fused_computation.1 | custom fusion | bytes 8390656 | tf_op jit(solution)/shard_map/gather | solution.py:40
  46.0 4.4 %gather_fusion = bf16[512,4096]{1,0:T(8,128)(2,1)} fusion(bf16[128,4096]{1,0:T(8,128)(2,1)S(1)} %copy-done.1, s32[1024]{0:T(1024)S(1)} %pad_clamp_fusion), kind=kCustom, calls=%fused_computation | custom fusion | bytes 8390656 | tf_op jit(solution)/shard_map/gather | solution.py:43
  50.4 5.8 %broadcast_select_fusion = (bf16[32,16,4096]{2,1,0:T(8,128)(2,1)}, bf16[32,16,4096]{2,1,0:T(8,128)(2,1)}) fusion(bf16[32,16,4096]{2,1,0:T(8,128)(2,1)} %bitcast.24, pred[32,16]{1,0:T(8,128)(4,1)S(1)} %broadcast_in_dim.63, bf16[32,16,4096]{2,1,0:T(8,128)(2,1)} %bitcast.25), kind=kLoop, calls=%fused_computation.16 | loop fusion | flops 4194304 | bytes 16777728 | tf_op jit(solution)/shard_map/jit(_where)/select_n | solution.py:40
  56.2 102.6 %all_to_all.29 = bf16[32,16,4096]{2,1,0:T(8,128)(2,1)} all-to-all(bf16[32,16,4096]{2,1,0:T(8,128)(2,1)} %get-tuple-element.17), channel_id=1, replica_groups=mesh['dp'=8,'expert'=32] {'expert'}, dimensions={0} | all-to-all | bytes 8388608 | tf_op jit(solution)/shard_map/all_to_all | solution.py:49
  158.8 6.7 %all-to-all-start.2 = ((bf16[32,16,4096]{2,1,0:T(8,128)(2,1)}), bf16[32,16,4096]{2,1,0:T(8,128)(2,1)}, u32[]{:S(2)}, u32[]{:S(2)}) async-start(bf16[32,16,4096]{2,1,0:T(8,128)(2,1)} %get-tuple-element.16), calls=%async_computation.3 | async-start | bytes 8388608 | tf_op jit(solution)/shard_map/all_to_all | solution.py:48
  166.0 7.7 %multiply_convert_fusion = bf16[512,768]{1,0:T(8,128)(2,1)S(1)} fusion(bf16[512,4096]{1,0:T(8,128)(2,1)} %bitcast.26, bf16[1,768,4096]{2,1,0:T(8,128)(2,1)} %param.13, f32[512]{0:T(512)S(1)} %reshape.110, bf16[512,768]{1,0:T(8,128)(2,1)S(1)} %copy-done.2), kind=kOutput, calls=%fused_computation.23 | convolution fusion | flops 3224371200 | bytes 12060672 | tf_op jit(solution)/shard_map/dot_general | solution.py:58
  173.6 84.6 %all-to-all-done.2 = bf16[32,16,4096]{2,1,0:T(8,128)(2,1)} async-done(((bf16[32,16,4096]{2,1,0:T(8,128)(2,1)}), bf16[32,16,4096]{2,1,0:T(8,128)(2,1)}, u32[]{:S(2)}, u32[]{:S(2)}) %all-to-all-start.2) | async-done | bytes 4194336 | tf_op jit(solution)/shard_map/all_to_all | solution.py:48
  258.3 8.3 %convolution_convert_fusion = bf16[4096,768]{1,0:T(8,128)(2,1)} fusion(bf16[512,4096]{1,0:T(8,128)(2,1)} %bitcast.6, bf16[512,768]{1,0:T(8,128)(2,1)S(1)} %multiply_convert_fusion), kind=kOutput, calls=%fused_computation.10 | convolution fusion | flops 3224371200 | bytes 11272192 | tf_op jit(solution)/shard_map/dot_general | solution.py:80
  266.6 1.1 copy-done.3
  267.7 9.1 %fusion.5 = f32[768,4096]{1,0:T(8,128)} fusion(bf16[512,4096]{1,0:T(8,128)(2,1)} %bitcast.27, f32[512]{0:T(512)S(1)} %reshape.110, bf16[512,768]{1,0:T(8,128)(2,1)S(1)} %copy-done.3, bf16[512,768]{1,0:T(8,128)(2,1)S(1)} %copy-done.2), kind=kOutput, calls=%fused_computation.14 | convolution fusion | flops 3230662656 | bytes 18352128 | tf_op jit(solution)/shard_map/dot_general | solution.py:72
  276.9 7.9 %fusion.1 = f32[512]{0:T(512)S(1)} fusion(bf16[512,4096]{1,0:T(8,128)(2,1)} %bitcast.28, bf16[1,768,4096]{2,1,0:T(8,128)(2,1)} %param.13, bf16[512,768]{1,0:T(8,128)(2,1)S(1)} %copy-done.3, bf16[512,768]{1,0:T(8,128)(2,1)S(1)} %copy-done.2), kind=kOutput, calls=%fused_computation.9 | convolution fusion | flops 3230662144 | bytes 12060672 | tf_op jit(solution)/shard_map/dot_general | solution.py:61
  284.8 0.7 all_to_all.22
  285.5 6.4 %all-to-all-start.3 = ((f32[32,1,16]{2,1,0:T(1,128)}), f32[32,1,16]{2,1,0:T(1,128)S(1)}, u32[]{:S(2)}, u32[]{:S(2)}) async-start(f32[32,1,16]{2,1,0:T(1,128)} %bitcast.9), calls=%async_computation.5 | async-start | bytes 32768 | tf_op jit(solution)/shard_map/all_to_all | solution.py:63
  292.0 8.6 %all-to-all-done.3 = f32[32,1,16]{2,1,0:T(1,128)S(1)} async-done(((f32[32,1,16]{2,1,0:T(1,128)}), f32[32,1,16]{2,1,0:T(1,128)S(1)}, u32[]{:S(2)}, u32[]{:S(2)}) %all-to-all-start.3) | async-done | bytes 2080 | tf_op jit(solution)/shard_map/all_to_all | solution.py:63
  301.9 6.9 %gather_fusion.2 = f32[1024]{0:T(1024)S(1)} fusion(f32[512]{0:T(512)S(1)} %reshape.109, s32[1024]{0:T(1024)S(1)} %broadcast_clamp_fusion), kind=kCustom, calls=%fused_computation.2 | custom fusion | bytes 12288 | tf_op jit(solution)/shard_map/gather | solution.py:66
  309.5 2.2 reduce-scatter.5.cloned.1.call-done
  311.7 78.2 %reduce-scatter.3.cloned.1.call-done = f32[96,4096]{1,0:T(8,128)} async-done(((f32[768,4096]{1,0:T(8,128)}), f32[96,4096]{1,0:T(8,128)}) %reduce-scatter.3.cloned.1.call-update) | async-done | bytes 1572880 | tf_op jit(solution)/shard_map/reduce_scatter | solution.py:71
  (42 shorter events, 3.8 us)
Async XLA Ops:
  7.2 34.5 %copy-start = (bf16[128,4096]{1,0:T(8,128)(2,1)S(1)}, bf16[128,4096]{1,0:T(8,128)(2,1)}, u32[]{:S(2)}) copy-start(bf16[128,4096]{1,0:T(8,128)(2,1)} %param.7) | copy-start | bytes 3145732
  25.3 31.0 %all-to-all-start = ((bf16[32,1,16]{2,1,0:T(2,128)(2,1)}), bf16[32,1,16]{2,1,0:T(2,128)(2,1)S(1)}, u32[]{:S(2)}, u32[]{:S(2)}) async-start(bf16[32,1,16]{2,1,0:T(2,128)(2,1)} %all_to_all.24), calls=%async_computation | async-start | bytes 32768 | tf_op jit(solution)/shard_map/all_to_all | solution.py:50
  41.7 4.4 %copy-start.1 = (bf16[128,4096]{1,0:T(8,128)(2,1)S(1)}, bf16[128,4096]{1,0:T(8,128)(2,1)}, u32[]{:S(2)}) copy-start(bf16[128,4096]{1,0:T(8,128)(2,1)} %param.8) | copy-start | bytes 3145732
  158.8 7.1 %copy-start.2 = (bf16[512,768]{1,0:T(8,128)(2,1)S(1)}, bf16[512,768]{1,0:T(8,128)(2,1)}, u32[]{:S(2)}) copy-start(bf16[512,768]{1,0:T(8,128)(2,1)} %param.11) | copy-start | bytes 2359300
  158.8 99.4 %all-to-all-start.2 = ((bf16[32,16,4096]{2,1,0:T(8,128)(2,1)}), bf16[32,16,4096]{2,1,0:T(8,128)(2,1)}, u32[]{:S(2)}, u32[]{:S(2)}) async-start(bf16[32,16,4096]{2,1,0:T(8,128)(2,1)} %get-tuple-element.16), calls=%async_computation.3 | async-start | bytes 8388608 | tf_op jit(solution)/shard_map/all_to_all | solution.py:48
  165.6 146.1 %reduce-scatter.5.cloned.1.call-start = ((), (), s32[]{:S(2)}) async-start(), calls=%async_computation.7 | async-start | bytes 7077888 | tf_op jit(solution)/shard_map/reduce_scatter | solution.py:83
  266.6 1.1 copy-start.3
  266.6 123.3 %reduce-scatter.3.cloned.1.call-start = ((), (), s32[]{:S(2)}) async-start(), calls=%async_computation.6 | async-start | bytes 14155776 | tf_op jit(solution)/shard_map/reduce_scatter | solution.py:71
  285.5 15.1 %all-to-all-start.3 = ((f32[32,1,16]{2,1,0:T(1,128)}), f32[32,1,16]{2,1,0:T(1,128)S(1)}, u32[]{:S(2)}, u32[]{:S(2)}) async-start(f32[32,1,16]{2,1,0:T(1,128)} %bitcast.9), calls=%async_computation.5 | async-start | bytes 32768 | tf_op jit(solution)/shard_map/all_to_all | solution.py:63
Sparse Core Ops, SparseCore 0:
  266.7 44.9 reduce-scatter.4
  314.9 74.9 reduce-scatter.2
where the time goes:
time: 397 us
  waiting for transfers between devices  174 us (44%)
  blocking collectives  103 us (26%)
  local copies, waits for them, and re-layouts  41 us (10%)
  matrix products  33 us (8%)
  starting transfers between devices  25.3 us (6%)
  between operations  14.2 us (4%)
  other arithmetic  7.02 us (2%)
    all_to_all x1, blocking collectives, per_device(): lax.all_to_all(send_dy, 'expert', split_axis=0, concat_axis=0, tiled=True)  103 us
    all_to_all x1, waiting for transfers between devices, per_device(): lax.all_to_all(send_x, 'expert', split_axis=0, concat_axis=0, tiled=True)  84.6 us
    reduce_scatter x1, waiting for transfers between devices, per_device(): lax.psum_scatter(lax.dot_general(column_block, scaled, (((0,), (0,)), (()...  78.2 us
    all_to_all x1, starting transfers between devices, per_device(): lax.all_to_all(send_weight, 'expert', split_axis=0, concat_axis=0, tiled=...  11.9 us
    dot_general x1, matrix products, per_device(): lax.dot_general(column_block, scaled, (((0,), (0,)), ((), ())), preferred...  9.07 us
    all_to_all x1, waiting for transfers between devices, per_device(): lax.all_to_all(slot_grad.reshape(owners, capacity), 'expert', split_axis=...  8.62 us
    dot_general x1, matrix products, per_device(): lax.dot_general(column_block, grad_pre, (((0,), (0,)), ((), ())), preferr...  8.29 us
  transfers between devices with their start and end apart: 5, of which 4 were waited for; matrix products, arithmetic and copies ran while one was open for 13% of the time, Pallas kernels for 0%

commit v1 on v0

v1 whole, which is shorter than its diff:
```python
import jax
import jax.numpy as jnp
from jax import lax
from jax.experimental import pallas as pl
from jax.experimental.pallas import tpu as pltpu
from jax.sharding import PartitionSpec as P

MESH = pl.DeviceIdType.MESH
NZ, NX, NY = 8, 4, 4
TOK = 128
CAP = 16
EXP_DEV = 4
D = 4096
FF = 768
NC = 4
DC = D // NC
UNITS = 2 * NC
ROWS = NX * CAP
SLOTS = NZ * ROWS
BLK = FF // (2 * NY)
F32 = jnp.float32
BF16 = jnp.bfloat16


def kernel(
    x_hbm, dy_hbm, probs_ref, routes_ref, gate_hbm, up_hbm, w_hbm,
    down_ref, upo_ref, pg_ref,
    tok, stg, recv, part, exr, yr, wv, gatev, hid, bg, lhs, sel, meta, metar, sg1, sg1r, sg2, sg2r,
    ld, zs, zr, xs, xr, es, er, ys, yrs, misc, cx, cy,
):
    dp = lax.axis_index("dp")
    e = lax.axis_index("expert")
    y, core = lax.div(dp, 2), lax.rem(dp, 2)
    z, x = lax.div(e, NX), lax.rem(e, NX)

    def at_z(zz):
        return (dp, lax.rem(zz, NZ) * NX + x)

    def at_x(xx):
        return (dp, z * NX + lax.rem(xx, NX))

    def at_y(yy):
        return (lax.rem(yy, NY) * 2 + core, e)

    partner = (y * 2 + 1 - core, e)

    def remote(src, dst, send, recv_sem, dev):
        return pltpu.make_async_remote_copy(
            src_ref=src, dst_ref=dst, send_sem=send, recv_sem=recv_sem,
            device_id=dev, device_id_type=MESH,
        )

    def drain(ref, sem):
        pltpu.make_async_copy(ref, ref, sem).wait()

    barrier = pltpu.get_barrier_semaphore()

    def greet(dev):
        pl.semaphore_signal(barrier, inc=1, device_id=dev, device_id_type=MESH)

    for i in range(1, NZ):
        greet(at_z(z + i))
    for i in range(1, NX):
        greet(at_x(x + i))
    for i in range(1, NY):
        greet(at_y(y + i))
    greet(partner)

    dy_loads = [
        pltpu.make_async_copy(dy_hbm.at[:, c * DC:(c + 1) * DC], tok.at[c, 0], ld.at[c])
        for c in range(NC)
    ]
    step = D // 8
    sub = step // NC
    x_loads = [
        pltpu.make_async_copy(
            x_hbm.at[:, d * step + c * sub:d * step + (c + 1) * sub],
            tok.at[NC + c, 0, :, d * sub:(d + 1) * sub],
            ld.at[NC + c],
        )
        for c in range(NC)
        for d in range(8)
    ]
    g_load = pltpu.make_async_copy(gate_hbm, gatev, ld.at[UNITS])
    u_load = pltpu.make_async_copy(up_hbm, hid, ld.at[UNITS + 1])
    w_load = pltpu.make_async_copy(w_hbm, wv, ld.at[UNITS + 2])
    for c in dy_loads:
        c.start()
    g_load.start()
    u_load.start()
    for c in x_loads:
        c.start()
    w_load.start()

    def zcopy(u, src, dst, sign):
        way = sign * (1 - 2 * lax.rem(u, 2))
        return remote(tok.at[u, src], tok.at[u, dst], zs.at[u], zr.at[u, dst], at_z(z + NZ + way))

    def send_own(u):
        zcopy(u, 0, 1, 1).start()
        zcopy(u, 0, NZ - 1, -1).start()

    r = routes_ref[...]
    p = probs_ref[...].astype(F32)
    owners = NZ * NX
    wid = lax.broadcasted_iota(jnp.int32, (owners, TOK), 0) * EXP_DEV
    routed = jnp.zeros((owners, TOK), F32)
    weight = jnp.zeros((owners, TOK), F32)
    for k in range(8):
        hit = wid == r[k:k + 1, :]
        routed = jnp.where(hit, 1.0, routed)
        weight = jnp.where(hit, p[k:k + 1, :], weight)
    earlier = lax.broadcasted_iota(jnp.int32, (TOK, TOK), 0) < lax.broadcasted_iota(
        jnp.int32, (TOK, TOK), 1
    )
    before = jnp.dot(
        routed.astype(BF16), jnp.where(earlier, 1.0, 0.0).astype(BF16), preferred_element_type=F32
    )
    pos = jnp.where((routed > 0.0) & (before < float(CAP)), before, -1.0)
    for i in range(NZ):
        meta[i, 0:NX, :] = pos[i * NX:(i + 1) * NX]
        meta[i, NX:2 * NX, :] = weight[i * NX:(i + 1) * NX]
    metar[z] = meta[z]

    pl.semaphore_wait(barrier, NZ + NX + NY - 2)
    dy_loads[0].wait()
    send_own(0)
    for i in range(1, NZ):
        to = lax.rem(z + i, NZ)
        remote(meta.at[to], metar.at[z], misc.at[0], misc.at[1], at_z(to)).start()
    dy_loads[1].wait()
    send_own(1)
    for c in dy_loads[2:]:
        c.wait()
    g_load.wait()
    u_load.wait()

    gate = gatev[...].astype(F32)
    act = gate / (1.0 + jnp.exp(-gate))
    hidden = (act * hid[...].astype(F32)).astype(BF16)
    hid[...] = hidden
    lhs[0] = hidden.T
    bg[...] = jnp.zeros_like(bg)
    for c in range(NC):
        drain(tok.at[NC + c, 0], ld.at[NC + c])
    w_load.wait()

    drain(metar.at[0:NZ - 1], misc.at[1])
    slot_pos = lax.broadcasted_iota(jnp.int32, (NX, CAP, TOK), 1).astype(F32)

    def build(src, carry):
        m = metar[src]
        at = m[0:NX].reshape(NX, 1, TOK)
        wt = m[NX:2 * NX].reshape(NX, 1, TOK)
        hit = jnp.broadcast_to(at, (NX, CAP, TOK)) == slot_pos
        one = jnp.where(hit, 1.0, 0.0)
        wtd = jnp.where(hit, jnp.broadcast_to(wt, (NX, CAP, TOK)), 0.0)
        sel[0, src] = wtd.reshape(ROWS, TOK).astype(BF16)
        sel[1, src] = one.reshape(ROWS, TOK).astype(BF16)
        return carry

    lax.fori_loop(0, NZ, build, 0)

    def select(u, j):
        way = 1 - 2 * lax.rem(u, 2)
        src = lax.rem(z + 8 * NZ - way * j, NZ)
        s = sel[lax.div(u, NC), src]
        rows = jnp.dot(s, tok[u, j], preferred_element_type=F32).astype(BF16)
        stg[u, j] = rows.reshape(NX, CAP, DC)
        slot = src * NX + x
        recv[u, slot] = stg[u, j, x]
        for i in range(1, NX):
            to = lax.rem(x + i, NX)
            remote(stg.at[u, j, to], recv.at[u, slot], xs.at[u], xr.at[u], at_x(to)).start()

    def on(k, t, body):
        u = k - t

        @pl.when((u >= 0) & (u < UNITS))
        def _():
            body(u)

    def relay1(u):
        drain(tok.at[u, 1], zr.at[u, 1])
        zcopy(u, 1, 2, 1).start()
        drain(tok.at[u, 7], zr.at[u, 7])
        zcopy(u, 7, 6, -1).start()

    def relay2(u):
        drain(tok.at[u, 2], zr.at[u, 2])
        zcopy(u, 2, 3, 1).start()
        drain(tok.at[u, 6], zr.at[u, 6])
        zcopy(u, 6, 5, -1).start()

    def relay3(u):
        drain(tok.at[u, 3], zr.at[u, 3])
        zcopy(u, 3, 4, 1).start()

    def pick1(u):
        select(u, 0)
        select(u, 1)
        select(u, 7)

    def pick2(u):
        select(u, 2)
        select(u, 6)

    def pick3(u):
        select(u, 3)
        drain(tok.at[u, 5], zr.at[u, 5])
        select(u, 5)

    def pick4(u):
        drain(tok.at[u, 4], zr.at[u, 4])
        select(u, 4)

    def compute(u):
        c = lax.rem(u, NC)
        kind = lax.div(u, NC)
        drain(recv.at[u, 0:NZ * (NX - 1)], xr.at[u])

        @pl.when(kind == 0)
        def _():
            a = recv[u].reshape(SLOTS, DC)
            wc = wv[:, pl.ds(pl.multiple_of(c * DC, DC), DC)]
            bg[...] += lax.dot_general(
                a, wc, (((1,), (1,)), ((), ())), preferred_element_type=F32
            )

        def tile(n, carry):
            cols = recv[u, :, :, pl.ds(pl.multiple_of(n * 256, 256), 256)].reshape(SLOTS, 256)
            prod = jnp.dot(lhs[kind], cols, preferred_element_type=F32).astype(BF16)

            @pl.when(kind == 0)
            def _():
                for d in range(2 * NY):
                    for h in range(2):
                        part[c, d % 2, d // 2, pl.ds(pl.multiple_of((2 * n + h) * BLK, BLK), BLK), :] = (
                            prod[d * BLK:(d + 1) * BLK, h * 128:(h + 1) * 128]
                        )

            @pl.when(kind == 1)
            def _():
                part[c, 0, n] = prod[:, 0:128]
                part[c, 1, n] = prod[:, 128:256]

            return carry

        lax.fori_loop(0, NY, tile, 0)

        @pl.when(kind == 1)
        def _():
            pl.semaphore_wait(cx.at[c], 1)

        remote(part.at[c, 1 - core], exr.at[c], es.at[u], er.at[u], partner).start()

        @pl.when(u == NC - 1)
        def _():
            back = bg[...]
            g = gatev[...].astype(F32)
            pre = (back * (g / (1.0 + jnp.exp(-g)))).astype(BF16)
            lhs[1] = pre.T
            sg = jnp.sum(hid[...].astype(F32) * back, axis=1, keepdims=True)
            lane = lax.broadcasted_iota(jnp.int32, (SLOTS, TOK), 1)
            row = lax.broadcasted_iota(jnp.int32, (SLOTS, TOK), 0)
            spread = jnp.where(lane == x * CAP + lax.rem(row, CAP), sg, 0.0)
            packed = jnp.sum(spread.reshape(NZ * NX, CAP, TOK), axis=1)
            for s in range(NZ * NX):
                sg1[s % NX, s // NX:s // NX + 1, :] = packed[s:s + 1, :]
            sg1r[x] = sg1[x]
            for i in range(1, NX):
                to = lax.rem(x + i, NX)
                remote(sg1.at[to], sg1r.at[x], misc.at[2], misc.at[3], at_x(to)).start()

    def chip_sum(u):
        c = lax.rem(u, NC)
        drain(exr.at[c], er.at[u])

        @pl.when(u >= NC)
        def _():
            pl.semaphore_wait(cy.at[c], NY - 1)

        for i in range(1, NY):
            to = lax.rem(y + i, NY)
            part[c, core, to] = (
                part[c, core, to].astype(F32) + exr[c, to].astype(F32)
            ).astype(BF16)
            remote(part.at[c, core, to], yr.at[c, i - 1], ys.at[u], yrs.at[u], at_y(to)).start()

    def finish(u):
        c = lax.rem(u, NC)
        drain(yr.at[c], yrs.at[u])
        total = part[c, core, y].astype(F32) + exr[c, y].astype(F32)
        for i in range(NY - 1):
            total = total + yr[c, i].astype(F32)

        @pl.when(u < NC)
        def _():
            for i in range(DC // 128):
                down_ref[:, pl.ds(pl.multiple_of(c * DC + i * 128, 128), 128)] = (
                    total[i * BLK:(i + 1) * BLK]
                )
            pl.semaphore_signal(cx.at[c], inc=1, device_id=partner, device_id_type=MESH)
            for i in range(1, NY):
                pl.semaphore_signal(cy.at[c], inc=1, device_id=at_y(y + i), device_id_type=MESH)

        @pl.when(u >= NC)
        def _():
            upo_ref[pl.ds(pl.multiple_of(c * 128, 128), 128), :] = total.T.astype(BF16)

        drain(tok.at[u, 0:NZ - 1], zs.at[u])
        drain(recv.at[u, 0:NZ * (NX - 1)], xs.at[u])
        drain(part.at[c, 0], es.at[u])
        drain(yr.at[c], ys.at[u])

    def grads_over_z():
        drain(sg1r.at[0:NX - 1], misc.at[3])
        both = sg1r[0] + sg1r[1] + sg1r[2] + sg1r[3]
        for i in range(NZ):
            sg2[i] = jnp.broadcast_to(both[i:i + 1, :], (8, TOK))
        sg2r[z] = sg2[z]
        for i in range(1, NZ):
            to = lax.rem(z + i, NZ)
            remote(sg2.at[to], sg2r.at[z], misc.at[4], misc.at[5], at_z(to)).start()

    def grads_out():
        drain(sg2r.at[0:NZ - 1], misc.at[5])
        eye = lax.broadcasted_iota(jnp.int32, (TOK, TOK), 0) == lax.broadcasted_iota(
            jnp.int32, (TOK, TOK), 1
        )
        rr = routes_ref[...]
        total = jnp.zeros((8, TOK), F32)
        for i in range(NZ):
            spread = jnp.where(eye, jnp.broadcast_to(sg2r[i, 0:1, :], (TOK, TOK)), 0.0)
            column = jnp.sum(spread, axis=1, keepdims=True)[0:ROWS].reshape(NX, CAP, 1)
            at = meta[i, 0:NX, :].reshape(NX, 1, TOK)
            hit = jnp.broadcast_to(at, (NX, CAP, TOK)) == slot_pos
            got = jnp.sum(jnp.where(hit, column, 0.0), axis=1)
            for j in range(NX):
                total = jnp.where(rr == (i * NX + j) * EXP_DEV, got[j:j + 1, :], total)
        pg_ref[...] = total / probs_ref[...].astype(F32)
        drain(meta.at[0:NZ - 1], misc.at[0])
        drain(sg1.at[0:NX - 1], misc.at[2])
        drain(sg2.at[0:NZ - 1], misc.at[4])

    def body(k, carry):
        @pl.when(k + 2 < UNITS)
        def _():
            send_own(k + 2)

        on(k, 1, relay1)
        on(k, 2, relay2)
        on(k, 3, relay3)
        on(k, 1, pick1)
        on(k, 2, pick2)
        on(k, 3, pick3)
        on(k, 4, pick4)
        on(k, 5, compute)
        on(k, 6, chip_sum)
        on(k, 7, finish)

        @pl.when(k == NC + 5)
        def _():
            grads_over_z()

        @pl.when(k == NC + 6)
        def _():
            grads_out()

        return carry

    lax.fori_loop(0, UNITS + 7, body, 0)


def per_device(tokens, out_grad, probs, routes, saved_gate, saved_up, down_weight):
    anyspace = pl.BlockSpec(memory_space=pl.ANY)
    vmem = pl.BlockSpec(memory_space=pltpu.VMEM)
    dma = pltpu.SemaphoreType.DMA
    down, up, pg = pl.pallas_call(
        kernel,
        out_shape=(
            jax.ShapeDtypeStruct((BLK, D), F32),
            jax.ShapeDtypeStruct((D // 8, FF), BF16),
            jax.ShapeDtypeStruct((8, TOK), F32),
        ),
        in_specs=[anyspace, anyspace, vmem, vmem, anyspace, anyspace, anyspace],
        out_specs=(vmem, vmem, vmem),
        scratch_shapes=[
            pltpu.VMEM((UNITS, NZ, TOK, DC), BF16),
            pltpu.VMEM((UNITS, NZ, NX, CAP, DC), BF16),
            pltpu.VMEM((UNITS, NZ * NX, CAP, DC), BF16),
            pltpu.VMEM((NC, 2, NY, FF, 128), BF16),
            pltpu.VMEM((NC, NY, FF, 128), BF16),
            pltpu.VMEM((NC, NY - 1, FF, 128), BF16),
            pltpu.VMEM((FF, D), BF16),
            pltpu.VMEM((SLOTS, FF), BF16),
            pltpu.VMEM((SLOTS, FF), BF16),
            pltpu.VMEM((SLOTS, FF), F32),
            pltpu.VMEM((2, FF, SLOTS), BF16),
            pltpu.VMEM((2, NZ, ROWS, TOK), BF16),
            pltpu.VMEM((NZ, 8, TOK), F32),
            pltpu.VMEM((NZ, 8, TOK), F32),
            pltpu.VMEM((NX, NZ, TOK), F32),
            pltpu.VMEM((NX, NZ, TOK), F32),
            pltpu.VMEM((NZ, 8, TOK), F32),
            pltpu.VMEM((NZ, 8, TOK), F32),
            dma((UNITS + 3,)),
            dma((UNITS,)),
            dma((UNITS, NZ)),
            dma((UNITS,)),
            dma((UNITS,)),
            dma((UNITS,)),
            dma((UNITS,)),
            dma((UNITS,)),
            dma((UNITS,)),
            dma((6,)),
            pltpu.SemaphoreType.REGULAR((NC,)),
            pltpu.SemaphoreType.REGULAR((NC,)),
        ],
        compiler_params=pltpu.CompilerParams(
            collective_id=0, has_side_effects=True, vmem_limit_bytes=67043328
        ),
        name="expert_grads",
    )(
        tokens, out_grad, probs.T, routes.T, saved_gate, saved_up,
        down_weight.reshape(down_weight.shape[1:]),
    )
    return down[None], up[None], pg.T


def solution(mesh):
    rows = P(("dp", "expert"), None)
    return jax.shard_map(
        per_device,
        mesh=mesh,
        in_specs=(rows, rows, rows, rows, rows, rows, P("expert", None, None)),
        out_specs=(P("expert", "dp", None), P("expert", "dp", None), rows),
        check_vma=False,
    )
```

time: 397 us -> 214 us (0.54)
  Pallas kernels: 0 us -> 209 us
  waiting for transfers between devices: 174 us -> 0 us
  blocking collectives: 103 us -> 0 us
  local copies, waits for them, and re-layouts: 41 us -> 4.2 us
  matrix products: 33 us -> 0 us
  starting transfers between devices: 25.3 us -> 0 us
  between operations: 14.2 us -> 0.66 us
  other arithmetic: 7.02 us -> 0 us
    pallas_call x0 -> x1, Pallas kernels: none -> 209 us  [per_device(): pl.pallas_call(kernel, out_shape=(jax.ShapeDtypeStruct((BLK, D), F32), ja...]
    all_to_all x1 -> x0, blocking collectives: 103 us -> none  [per_device(): lax.all_to_all(send_dy, 'expert', split_axis=0, concat_axis=0, tiled=True)]
    all_to_all x3 -> x0, waiting for transfers between devices: 93.3 us -> none  [the longest x1 84.6 us: per_device(): lax.all_to_all(send_x, 'expert', split_axis=0, concat_axis=0, tiled=True)]
    reduce_scatter x2 -> x0, waiting for transfers between devices: 80.4 us -> none  [the longest x1 78.2 us: per_device(): lax.psum_scatter(lax.dot_general(column_block, scaled, (((0,), (0,)), (()...]
    dot_general x4 -> x0, matrix products: 33 us -> none  [the longest x1 9.07 us: per_device(): lax.dot_general(column_block, scaled, (((0,), (0,)), ((), ())), preferred...]
    all_to_all x3 -> x0, starting transfers between devices: 25 us -> none  [the longest x1 11.9 us: per_device(): lax.all_to_all(send_weight, 'expert', split_axis=0, concat_axis=0, tiled=...]
    gather x7 -> x0, local copies, waits for them, and re-layouts: 22.9 us -> none  [the longest x3 7.26 us: per_device(): position = jnp.take_along_axis(before, target, axis=1)]
    scatter x2 -> x0, local copies, waits for them, and re-layouts: 11.9 us -> none  [the longest x1 7.58 us: per_device(): jnp.zeros((slot_rows,), jnp.bfloat16).at[flat_index]]
  transfers between devices with their start and end apart: 5 -> 0, of which waited for: 4 -> 0; matrix products, arithmetic and copies ran while one was open for 13% -> 0% of each run, Pallas kernels for 0% -> 0%
where the time goes in v1:
time: 214 us
  Pallas kernels  209 us (98%)
  local copies, waits for them, and re-layouts  4.2 us (2%)
    pallas_call x1, Pallas kernels, per_device(): pl.pallas_call(kernel, out_shape=(jax.ShapeDtypeStruct((BLK, D), F32), ja...  209 us

profile of v1, /device:TPU:1, one launch (start us, length us, event | category | flops | bytes accessed | tf_op | source)
XLA Modules:
  0.0 213.8 jit_solution(14839844578827422544)
XLA Ops:
  0.6 209.0 %expert_grads.1 = (f32[96,4096]{1,0:T(8,128)}, bf16[512,768]{1,0:T(8,128)(2,1)}, f32[8,128]{1,0:T(8,128)}) custom-call(bf16[128,4096]{1,0:T(8,128)(2,1)} %x_hbm.1, bf16[128,4096]{1,0:T(8,128)(2,1)} %dy_hbm.1, bf16[8,128]{1,0:T(8,128)(2,1)} %bitcast.11, s32[8,128]{1,0:T(8,128)} %bitcast.9, bf16[512,768]{1,0:T(8,128)(2,1)} %gate_hbm.1, ...), custom_call_target="tpu_custom_call" | custom-call | tf_op jit(solution)/shard_map/expert_grads/pallas_call | solution.py:379
  209.6 0.0 copy-start
  209.6 0.0 copy-start.1
  209.6 2.7 %copy.13 = f32[1,96,4096]{2,1,0:T(8,128)} copy(f32[1,96,4096]{2,1,0:T(8,128)} %bitcast.7) | data formatting | bytes 3145728
  212.4 0.0 copy-done
  212.4 0.9 copy.14
  213.2 0.0 copy-done.1
  213.2 0.6 copy.15
Async XLA Ops:
  209.6 2.7 %copy-start = (bf16[512,768]{1,0:T(8,128)(2,1)S(1)}, bf16[512,768]{1,0:T(8,128)(2,1)}, u32[]{:S(2)}) copy-start(bf16[512,768]{1,0:T(8,128)(2,1)} %get-tuple-element.7) | copy-start | bytes 2359300
  209.6 3.6 %copy-start.1 = (f32[8,128]{1,0:T(8,128)S(1)}, f32[8,128]{1,0:T(8,128)}, u32[]{:S(2)}) copy-start(f32[8,128]{1,0:T(8,128)} %get-tuple-element.8) | copy-start | bytes 12292

commit v2 on v1

--- a/solution.py
+++ b/solution.py
@@ -12,21 +12,23 @@
 EXP_DEV = 4
 D = 4096
 FF = 768
-NC = 4
+NC = 8
 DC = D // NC
 UNITS = 2 * NC
 ROWS = NX * CAP
 SLOTS = NZ * ROWS
 BLK = FF // (2 * NY)
+HALF = FF // 2
+AHEAD = 2
 F32 = jnp.float32
 BF16 = jnp.bfloat16
 
 
 def kernel(
     x_hbm, dy_hbm, probs_ref, routes_ref, gate_hbm, up_hbm, w_hbm,
-    down_ref, upo_ref, pg_ref,
-    tok, stg, recv, part, exr, yr, wv, gatev, hid, bg, lhs, sel, meta, metar, sg1, sg1r, sg2, sg2r,
-    ld, zs, zr, xs, xr, es, er, ys, yrs, misc, cx, cy,
+    down_hbm, up_out, pg_ref,
+    tok, far, stg, stf, recv, part, exr, yr, wv, gatev, hid, bg, lhs, sel, meta, metar, metaf, sg1, sg1r, sg2, sg2r,
+    down_ref, upo_ref, ld, od, zs, zr, xs, xr, es, er, ys, yrs, misc, cx, cy,
 ):
     dp = lax.axis_index("dp")
     e = lax.axis_index("expert")
@@ -71,15 +73,14 @@
         for c in range(NC)
     ]
     step = D // 8
-    sub = step // NC
     x_loads = [
         pltpu.make_async_copy(
-            x_hbm.at[:, d * step + c * sub:d * step + (c + 1) * sub],
-            tok.at[NC + c, 0, :, d * sub:(d + 1) * sub],
+            x_hbm.at[:, (2 * i + c % 2) * step + c // 2 * 128:(2 * i + c % 2) * step + (c // 2 + 1) * 128],
+            tok.at[NC + c, 0, :, i * 128:(i + 1) * 128],
             ld.at[NC + c],
         )
         for c in range(NC)
-        for d in range(8)
+        for i in range(NY)
     ]
     g_load = pltpu.make_async_copy(gate_hbm, gatev, ld.at[UNITS])
     u_load = pltpu.make_async_copy(up_hbm, hid, ld.at[UNITS + 1])
@@ -96,9 +97,18 @@
         way = sign * (1 - 2 * lax.rem(u, 2))
         return remote(tok.at[u, src], tok.at[u, dst], zs.at[u], zr.at[u, dst], at_z(z + NZ + way))
 
+    def zfar(u, src, dst, sign):
+        way = sign * (1 - 2 * lax.rem(u, 2))
+        i = dst - 4
+        c = lax.rem(u, NC)
+        s = sel[lax.div(u, NC), NZ + 2 * lax.rem(u, 2) + i]
+        rows = jnp.dot(s, tok[u, src], preferred_element_type=F32).astype(BF16)
+        far[c, i] = rows.reshape(NX, CAP, DC)
+        remote(far.at[c, i], stf.at[u, i], zs.at[u], zr.at[u, 2 + dst], at_z(z + NZ + way)).start()
+
     def send_own(u):
         zcopy(u, 0, 1, 1).start()
-        zcopy(u, 0, NZ - 1, -1).start()
+        zcopy(u, 0, 5, -1).start()
 
     r = routes_ref[...]
     p = probs_ref[...].astype(F32)
@@ -123,15 +133,16 @@
     metar[z] = meta[z]
 
     pl.semaphore_wait(barrier, NZ + NX + NY - 2)
-    dy_loads[0].wait()
-    send_own(0)
     for i in range(1, NZ):
         to = lax.rem(z + i, NZ)
         remote(meta.at[to], metar.at[z], misc.at[0], misc.at[1], at_z(to)).start()
-    dy_loads[1].wait()
-    send_own(1)
-    for c in dy_loads[2:]:
-        c.wait()
+    for i, (node, plane) in enumerate(((3, 4), (6, 5), (5, 4), (2, 3))):
+        plane = lax.rem(z + plane, NZ)
+        remote(meta.at[plane], metaf.at[i], misc.at[6], misc.at[7], at_z(z + node)).start()
+    for c in range(NC):
+        dy_loads[c].wait()
+        if c < max(AHEAD, 1):
+            send_own(c)
     g_load.wait()
     u_load.wait()
 
@@ -146,32 +157,41 @@
     w_load.wait()
 
     drain(metar.at[0:NZ - 1], misc.at[1])
+    drain(metaf, misc.at[7])
     slot_pos = lax.broadcasted_iota(jnp.int32, (NX, CAP, TOK), 1).astype(F32)
 
-    def build(src, carry):
-        m = metar[src]
+    def build(m, i):
         at = m[0:NX].reshape(NX, 1, TOK)
         wt = m[NX:2 * NX].reshape(NX, 1, TOK)
         hit = jnp.broadcast_to(at, (NX, CAP, TOK)) == slot_pos
         one = jnp.where(hit, 1.0, 0.0)
         wtd = jnp.where(hit, jnp.broadcast_to(wt, (NX, CAP, TOK)), 0.0)
-        sel[0, src] = wtd.reshape(ROWS, TOK).astype(BF16)
-        sel[1, src] = one.reshape(ROWS, TOK).astype(BF16)
-        return carry
-
-    lax.fori_loop(0, NZ, build, 0)
-
-    def select(u, j):
+        sel[0, i] = wtd.reshape(ROWS, TOK).astype(BF16)
+        sel[1, i] = one.reshape(ROWS, TOK).astype(BF16)
+
+    for i in range(NZ):
+        build(metar[i], i)
+    for i in range(4):
+        build(metaf[i], NZ + i)
+
+    def pick(u, j):
         way = 1 - 2 * lax.rem(u, 2)
         src = lax.rem(z + 8 * NZ - way * j, NZ)
+        c = lax.rem(u, NC)
+        i = j if j < 4 else j - 2
         s = sel[lax.div(u, NC), src]
-        rows = jnp.dot(s, tok[u, j], preferred_element_type=F32).astype(BF16)
-        stg[u, j] = rows.reshape(NX, CAP, DC)
+        rows = jnp.dot(s, tok[u, i], preferred_element_type=F32).astype(BF16)
+        stg[c, i] = rows.reshape(NX, CAP, DC)
+        spread(u, j, stg.at[c, i])
+
+    def spread(u, j, ref):
+        way = 1 - 2 * lax.rem(u, 2)
+        src = lax.rem(z + 8 * NZ - way * j, NZ)
         slot = src * NX + x
-        recv[u, slot] = stg[u, j, x]
+        recv[u, slot] = ref[x]
         for i in range(1, NX):
             to = lax.rem(x + i, NX)
-            remote(stg.at[u, j, to], recv.at[u, slot], xs.at[u], xr.at[u], at_x(to)).start()
+            remote(ref.at[to], recv.at[u, slot], xs.at[u], xr.at[u], at_x(to)).start()
 
     def on(k, t, body):
         u = k - t
@@ -183,36 +203,36 @@
     def relay1(u):
         drain(tok.at[u, 1], zr.at[u, 1])
         zcopy(u, 1, 2, 1).start()
-        drain(tok.at[u, 7], zr.at[u, 7])
-        zcopy(u, 7, 6, -1).start()
+        drain(tok.at[u, 5], zr.at[u, 5])
+        zcopy(u, 5, 4, -1).start()
 
     def relay2(u):
         drain(tok.at[u, 2], zr.at[u, 2])
         zcopy(u, 2, 3, 1).start()
-        drain(tok.at[u, 6], zr.at[u, 6])
-        zcopy(u, 6, 5, -1).start()
+        drain(tok.at[u, 4], zr.at[u, 4])
+        zfar(u, 4, 5, -1)
 
     def relay3(u):
         drain(tok.at[u, 3], zr.at[u, 3])
-        zcopy(u, 3, 4, 1).start()
+        zfar(u, 3, 4, 1)
 
     def pick1(u):
-        select(u, 0)
-        select(u, 1)
-        select(u, 7)
+        pick(u, 0)
+        pick(u, 1)
+        pick(u, 7)
 
     def pick2(u):
-        select(u, 2)
-        select(u, 6)
+        pick(u, 2)
+        pick(u, 6)
 
     def pick3(u):
-        select(u, 3)
-        drain(tok.at[u, 5], zr.at[u, 5])
-        select(u, 5)
+        pick(u, 3)
+        drain(stf.at[u, 1], zr.at[u, 7])
+        spread(u, 5, stf.at[u, 1])
 
     def pick4(u):
-        drain(tok.at[u, 4], zr.at[u, 4])
-        select(u, 4)
+        drain(stf.at[u, 0], zr.at[u, 6])
+        spread(u, 4, stf.at[u, 0])
 
     def compute(u):
         c = lax.rem(u, NC)
@@ -235,24 +255,39 @@
             def _():
                 for d in range(2 * NY):
                     for h in range(2):
-                        part[c, d % 2, d // 2, pl.ds(pl.multiple_of((2 * n + h) * BLK, BLK), BLK), :] = (
+                        part[c, d % 2 * NY + d // 2, pl.ds(pl.multiple_of((2 * n + h) * BLK, BLK), BLK), :] = (
                             prod[d * BLK:(d + 1) * BLK, h * 128:(h + 1) * 128]
                         )
 
             @pl.when(kind == 1)
             def _():
-                part[c, 0, n] = prod[:, 0:128]
-                part[c, 1, n] = prod[:, 128:256]
+                for i in range(2):
+                    for h in range(2):
+                        part[c, 4 * n + 2 * i + h] = (
+                            prod[h * HALF:(h + 1) * HALF, i * 128:(i + 1) * 128]
+                        )
+
+                @pl.when(core != lax.rem(c, 2))
+                def _():
+                    for i in range(2):
+                        m = 2 * n + i
+                        ref = pl.ds(2 * m, 2)
+                        remote(part.at[c, ref], exr.at[c, ref], es.at[u], er.at[u, m], partner).start()
 
             return carry
 
-        lax.fori_loop(0, NY, tile, 0)
-
         @pl.when(kind == 1)
         def _():
             pl.semaphore_wait(cx.at[c], 1)
 
-        remote(part.at[c, 1 - core], exr.at[c], es.at[u], er.at[u], partner).start()
+        lax.fori_loop(0, DC // 256, tile, 0)
+
+        @pl.when(kind == 0)
+        def _():
+            for m in range(NY):
+                remote(
+                    part.at[c, (1 - core) * NY + m], exr.at[c, m], es.at[u], er.at[u, m], partner
+                ).start()
 
         @pl.when(u == NC - 1)
         def _():
@@ -274,44 +309,74 @@
 
     def chip_sum(u):
         c = lax.rem(u, NC)
-        drain(exr.at[c], er.at[u])
+        drain(tok.at[u, 0:6], zs.at[u])
+        drain(recv.at[u, 0:NZ * (NX - 1)], xs.at[u])
+
+        @pl.when(u < NC)
+        def _():
+            for i in (2, 3, 1):
+                to = lax.rem(y + i, NY)
+                mine = core * NY + to
+                drain(exr.at[c, to], er.at[u, to])
+                part[c, mine] = (part[c, mine].astype(F32) + exr[c, to].astype(F32)).astype(BF16)
+                remote(part.at[c, mine], yr.at[c, i - 1, 0], ys.at[u], yrs.at[u], at_y(to)).start()
 
         @pl.when(u >= NC)
         def _():
             pl.semaphore_wait(cy.at[c], NY - 1)
 
-        for i in range(1, NY):
-            to = lax.rem(y + i, NY)
-            part[c, core, to] = (
-                part[c, core, to].astype(F32) + exr[c, to].astype(F32)
-            ).astype(BF16)
-            remote(part.at[c, core, to], yr.at[c, i - 1], ys.at[u], yrs.at[u], at_y(to)).start()
+        @pl.when((u >= NC) & (core == lax.rem(c, 2)))
+        def _():
+            for i in (2, 3, 1):
+                to = lax.rem(y + i, NY)
+                ref = pl.ds(2 * to, 2)
+                drain(exr.at[c, ref], er.at[u, to])
+                for h in range(2):
+                    m = 2 * to + h
+                    part[c, m] = (part[c, m].astype(F32) + exr[c, m].astype(F32)).astype(BF16)
+                remote(part.at[c, ref], yr.at[c, i - 1], ys.at[u], yrs.at[u], at_y(to)).start()
 
     def finish(u):
         c = lax.rem(u, NC)
-        drain(yr.at[c], yrs.at[u])
-        total = part[c, core, y].astype(F32) + exr[c, y].astype(F32)
-        for i in range(NY - 1):
-            total = total + yr[c, i].astype(F32)
+        own = core == lax.rem(c, 2)
 
         @pl.when(u < NC)
         def _():
+            drain(exr.at[c, y], er.at[u, y])
+            drain(part.at[c, 0:NY - 1], yrs.at[u])
+            total = part[c, core * NY + y].astype(F32) + exr[c, y].astype(F32)
+            for i in range(NY - 1):
+                total = total + yr[c, i, 0].astype(F32)
             for i in range(DC // 128):
                 down_ref[:, pl.ds(pl.multiple_of(c * DC + i * 128, 128), 128)] = (
                     total[i * BLK:(i + 1) * BLK]
                 )
+            cols = pl.ds(pl.multiple_of(c * DC, DC), DC)
+            pltpu.make_async_copy(down_ref.at[:, cols], down_hbm.at[:, cols], od.at[u]).start()
             pl.semaphore_signal(cx.at[c], inc=1, device_id=partner, device_id_type=MESH)
             for i in range(1, NY):
                 pl.semaphore_signal(cy.at[c], inc=1, device_id=at_y(y + i), device_id_type=MESH)
-
-        @pl.when(u >= NC)
-        def _():
-            upo_ref[pl.ds(pl.multiple_of(c * 128, 128), 128), :] = total.T.astype(BF16)
-
-        drain(tok.at[u, 0:NZ - 1], zs.at[u])
-        drain(recv.at[u, 0:NZ * (NX - 1)], xs.at[u])
-        drain(part.at[c, 0], es.at[u])
-        drain(yr.at[c], ys.at[u])
+            drain(part.at[c, 0:NY], es.at[u])
+            drain(part.at[c, 0:NY - 1], ys.at[u])
+
+        @pl.when((u >= NC) & own)
+        def _():
+            drain(exr.at[c, pl.ds(2 * y, 2)], er.at[u, y])
+            drain(yr.at[c], yrs.at[u])
+            for h in range(2):
+                total = part[c, 2 * y + h].astype(F32) + exr[c, 2 * y + h].astype(F32)
+                for i in range(NY - 1):
+                    total = total + yr[c, i, h].astype(F32)
+                upo_ref[
+                    pl.ds(pl.multiple_of(lax.div(c, 2) * 128, 128), 128), h * HALF:(h + 1) * HALF
+                ] = total.T.astype(BF16)
+            out = pl.ds(pl.multiple_of(lax.div(c, 2) * 128, 128), 128)
+            pltpu.make_async_copy(upo_ref.at[out], up_out.at[out], od.at[u]).start()
+            drain(yr.at[c], ys.at[u])
+
+        @pl.when((u >= NC) & (core != lax.rem(c, 2)))
+        def _():
+            drain(part.at[c], es.at[u])
 
     def grads_over_z():
         drain(sg1r.at[0:NX - 1], misc.at[3])
@@ -340,13 +405,14 @@
                 total = jnp.where(rr == (i * NX + j) * EXP_DEV, got[j:j + 1, :], total)
         pg_ref[...] = total / probs_ref[...].astype(F32)
         drain(meta.at[0:NZ - 1], misc.at[0])
+        drain(metaf, misc.at[6])
         drain(sg1.at[0:NX - 1], misc.at[2])
         drain(sg2.at[0:NZ - 1], misc.at[4])
 
     def body(k, carry):
-        @pl.when(k + 2 < UNITS)
-        def _():
-            send_own(k + 2)
+        @pl.when((k + AHEAD < UNITS) & (k + AHEAD > 0))
+        def _():
+            send_own(k + AHEAD)
 
         on(k, 1, relay1)
         on(k, 2, relay2)
@@ -356,8 +422,8 @@
         on(k, 3, pick3)
         on(k, 4, pick4)
         on(k, 5, compute)
-        on(k, 6, chip_sum)
-        on(k, 7, finish)
+        on(k, 7, chip_sum)
+        on(k, 9, finish)
 
         @pl.when(k == NC + 5)
         def _():
@@ -369,7 +435,11 @@
 
         return carry
 
-    lax.fori_loop(0, UNITS + 7, body, 0)
+    lax.fori_loop(0, UNITS + 9, body, 0)
+    for c in range(NC):
+        drain(down_ref.at[:, c * DC:(c + 1) * DC], od.at[c])
+    for q in range(NC // 2):
+        drain(upo_ref.at[q * 128:(q + 1) * 128], od.at[NC + 2 * q + core])
 
 
 def per_device(tokens, out_grad, probs, routes, saved_gate, saved_up, down_weight):
@@ -384,36 +454,42 @@
             jax.ShapeDtypeStruct((8, TOK), F32),
         ),
         in_specs=[anyspace, anyspace, vmem, vmem, anyspace, anyspace, anyspace],
-        out_specs=(vmem, vmem, vmem),
+        out_specs=(anyspace, anyspace, vmem),
         scratch_shapes=[
-            pltpu.VMEM((UNITS, NZ, TOK, DC), BF16),
-            pltpu.VMEM((UNITS, NZ, NX, CAP, DC), BF16),
+            pltpu.VMEM((UNITS, 6, TOK, DC), BF16),
+            pltpu.VMEM((NC, 2, NX, CAP, DC), BF16),
+            pltpu.VMEM((NC, 6, NX, CAP, DC), BF16),
+            pltpu.VMEM((UNITS, 2, NX, CAP, DC), BF16),
             pltpu.VMEM((UNITS, NZ * NX, CAP, DC), BF16),
-            pltpu.VMEM((NC, 2, NY, FF, 128), BF16),
-            pltpu.VMEM((NC, NY, FF, 128), BF16),
-            pltpu.VMEM((NC, NY - 1, FF, 128), BF16),
+            pltpu.VMEM((NC, 2 * NY, HALF, 128), BF16),
+            pltpu.VMEM((NC, 2 * NY, HALF, 128), BF16),
+            pltpu.VMEM((NC, NY - 1, 2, HALF, 128), BF16),
             pltpu.VMEM((FF, D), BF16),
             pltpu.VMEM((SLOTS, FF), BF16),
             pltpu.VMEM((SLOTS, FF), BF16),
             pltpu.VMEM((SLOTS, FF), F32),
             pltpu.VMEM((2, FF, SLOTS), BF16),
-            pltpu.VMEM((2, NZ, ROWS, TOK), BF16),
+            pltpu.VMEM((2, NZ + 4, ROWS, TOK), BF16),
             pltpu.VMEM((NZ, 8, TOK), F32),
             pltpu.VMEM((NZ, 8, TOK), F32),
+            pltpu.VMEM((4, 8, TOK), F32),
             pltpu.VMEM((NX, NZ, TOK), F32),
             pltpu.VMEM((NX, NZ, TOK), F32),
             pltpu.VMEM((NZ, 8, TOK), F32),
             pltpu.VMEM((NZ, 8, TOK), F32),
+            pltpu.VMEM((BLK, D), F32),
+            pltpu.VMEM((D // 8, FF), BF16),
             dma((UNITS + 3,)),
             dma((UNITS,)),
+            dma((UNITS,)),
             dma((UNITS, NZ)),
             dma((UNITS,)),
             dma((UNITS,)),
             dma((UNITS,)),
-            dma((UNITS,)),
-            dma((UNITS,)),
-            dma((UNITS,)),
-            dma((6,)),
+            dma((UNITS, NY)),
+            dma((UNITS,)),
+            dma((UNITS,)),
+            dma((8,)),
             pltpu.SemaphoreType.REGULAR((NC,)),
             pltpu.SemaphoreType.REGULAR((NC,)),
         ],

time: 214 us -> 188 us (0.88)
  Pallas kernels: 209 us -> 183 us
    pallas_call x1, Pallas kernels: 209 us -> 183 us  [per_device(): pl.pallas_call(kernel, out_shape=(jax.ShapeDtypeStruct((BLK, D), F32), ja...]
where the time goes in v2:
time: 188 us
  Pallas kernels  183 us (97%)
  local copies, waits for them, and re-layouts  4.2 us (2%)
    pallas_call x1, Pallas kernels, per_device(): pl.pallas_call(kernel, out_shape=(jax.ShapeDtypeStruct((BLK, D), F32), ja...  183 us
    unnamed x7, local copies, waits for them, and re-layouts  4.2 us

profile of v2, /device:TPU:1, one launch (start us, length us, event | category | flops | bytes accessed | tf_op | source)
XLA Modules:
  0.0 187.5 jit_solution(7825451129747079976)
XLA Ops:
  0.6 182.6 %expert_grads.1 = (f32[96,4096]{1,0:T(8,128)}, bf16[512,768]{1,0:T(8,128)(2,1)}, f32[8,128]{1,0:T(8,128)}) custom-call(bf16[128,4096]{1,0:T(8,128)(2,1)} %x_hbm.1, bf16[128,4096]{1,0:T(8,128)(2,1)} %dy_hbm.1, bf16[8,128]{1,0:T(8,128)(2,1)} %bitcast.11, s32[8,128]{1,0:T(8,128)} %bitcast.9, bf16[512,768]{1,0:T(8,128)(2,1)} %gate_hbm.1, ...), custom_call_target="tpu_custom_call" | custom-call | tf_op jit(solution)/shard_map/expert_grads/pallas_call | solution.py:449
  183.3 0.0 copy-start
  183.3 0.0 copy-start.1
  183.3 2.7 %copy.13 = f32[1,96,4096]{2,1,0:T(8,128)} copy(f32[1,96,4096]{2,1,0:T(8,128)} %bitcast.7) | data formatting | bytes 3145728
  186.0 0.0 copy-done
  186.0 0.9 copy.14
  186.9 0.0 copy-done.1
  186.9 0.6 copy.15
Async XLA Ops:
  183.3 2.7 %copy-start = (bf16[512,768]{1,0:T(8,128)(2,1)S(1)}, bf16[512,768]{1,0:T(8,128)(2,1)}, u32[]{:S(2)}) copy-start(bf16[512,768]{1,0:T(8,128)(2,1)} %get-tuple-element.7) | copy-start | bytes 2359300
  183.3 3.6 %copy-start.1 = (f32[8,128]{1,0:T(8,128)S(1)}, f32[8,128]{1,0:T(8,128)}, u32[]{:S(2)}) copy-start(f32[8,128]{1,0:T(8,128)} %get-tuple-element.8) | copy-start | bytes 12292

commit v3 on v2

--- a/solution.py
+++ b/solution.py
@@ -77,14 +77,14 @@
         pltpu.make_async_copy(
             x_hbm.at[:, (2 * i + c % 2) * step + c // 2 * 128:(2 * i + c % 2) * step + (c // 2 + 1) * 128],
             tok.at[NC + c, 0, :, i * 128:(i + 1) * 128],
-            ld.at[NC + c],
+            ld.at[NC + 3],
         )
         for c in range(NC)
         for i in range(NY)
     ]
-    g_load = pltpu.make_async_copy(gate_hbm, gatev, ld.at[UNITS])
-    u_load = pltpu.make_async_copy(up_hbm, hid, ld.at[UNITS + 1])
-    w_load = pltpu.make_async_copy(w_hbm, wv, ld.at[UNITS + 2])
+    g_load = pltpu.make_async_copy(gate_hbm, gatev, ld.at[NC])
+    u_load = pltpu.make_async_copy(up_hbm, hid, ld.at[NC + 1])
+    w_load = pltpu.make_async_copy(w_hbm, wv, ld.at[NC + 2])
     for c in dy_loads:
         c.start()
     g_load.start()
@@ -95,7 +95,7 @@
 
     def zcopy(u, src, dst, sign):
         way = sign * (1 - 2 * lax.rem(u, 2))
-        return remote(tok.at[u, src], tok.at[u, dst], zs.at[u], zr.at[u, dst], at_z(z + NZ + way))
+        return remote(tok.at[u, src], tok.at[u, dst], zs.at[lax.rem(u, NC)], zr.at[lax.rem(u, NC), dst], at_z(z + NZ + way))
 
     def zfar(u, src, dst, sign):
         way = sign * (1 - 2 * lax.rem(u, 2))
@@ -104,7 +104,7 @@
         s = sel[lax.div(u, NC), NZ + 2 * lax.rem(u, 2) + i]
         rows = jnp.dot(s, tok[u, src], preferred_element_type=F32).astype(BF16)
         far[c, i] = rows.reshape(NX, CAP, DC)
-        remote(far.at[c, i], stf.at[u, i], zs.at[u], zr.at[u, 2 + dst], at_z(z + NZ + way)).start()
+        remote(far.at[c, i], stf.at[u, i], zs.at[lax.rem(u, NC)], zr.at[lax.rem(u, NC), 2 + dst], at_z(z + NZ + way)).start()
 
     def send_own(u):
         zcopy(u, 0, 1, 1).start()
@@ -152,8 +152,7 @@
     hid[...] = hidden
     lhs[0] = hidden.T
     bg[...] = jnp.zeros_like(bg)
-    for c in range(NC):
-        drain(tok.at[NC + c, 0], ld.at[NC + c])
+    drain(x_hbm, ld.at[NC + 3])
     w_load.wait()
 
     drain(metar.at[0:NZ - 1], misc.at[1])
@@ -191,7 +190,7 @@
         recv[u, slot] = ref[x]
         for i in range(1, NX):
             to = lax.rem(x + i, NX)
-            remote(ref.at[to], recv.at[u, slot], xs.at[u], xr.at[u], at_x(to)).start()
+            remote(ref.at[to], recv.at[u, slot], xs.at[lax.rem(u, NC)], xr.at[lax.rem(u, NC)], at_x(to)).start()
 
     def on(k, t, body):
         u = k - t
@@ -201,19 +200,19 @@
             body(u)
 
     def relay1(u):
-        drain(tok.at[u, 1], zr.at[u, 1])
+        drain(tok.at[u, 1], zr.at[lax.rem(u, NC), 1])
         zcopy(u, 1, 2, 1).start()
-        drain(tok.at[u, 5], zr.at[u, 5])
+        drain(tok.at[u, 5], zr.at[lax.rem(u, NC), 5])
         zcopy(u, 5, 4, -1).start()
 
     def relay2(u):
-        drain(tok.at[u, 2], zr.at[u, 2])
+        drain(tok.at[u, 2], zr.at[lax.rem(u, NC), 2])
         zcopy(u, 2, 3, 1).start()
-        drain(tok.at[u, 4], zr.at[u, 4])
+        drain(tok.at[u, 4], zr.at[lax.rem(u, NC), 4])
         zfar(u, 4, 5, -1)
 
     def relay3(u):
-        drain(tok.at[u, 3], zr.at[u, 3])
+        drain(tok.at[u, 3], zr.at[lax.rem(u, NC), 3])
         zfar(u, 3, 4, 1)
 
     def pick1(u):
@@ -227,17 +226,17 @@
 
     def pick3(u):
         pick(u, 3)
-        drain(stf.at[u, 1], zr.at[u, 7])
+        drain(stf.at[u, 1], zr.at[lax.rem(u, NC), 7])
         spread(u, 5, stf.at[u, 1])
 
     def pick4(u):
-        drain(stf.at[u, 0], zr.at[u, 6])
+        drain(stf.at[u, 0], zr.at[lax.rem(u, NC), 6])
         spread(u, 4, stf.at[u, 0])
 
     def compute(u):
         c = lax.rem(u, NC)
         kind = lax.div(u, NC)
-        drain(recv.at[u, 0:NZ * (NX - 1)], xr.at[u])
+        drain(recv.at[u, 0:NZ * (NX - 1)], xr.at[lax.rem(u, NC)])
 
         @pl.when(kind == 0)
         def _():
@@ -272,7 +271,7 @@
                     for i in range(2):
                         m = 2 * n + i
                         ref = pl.ds(2 * m, 2)
-                        remote(part.at[c, ref], exr.at[c, ref], es.at[u], er.at[u, m], partner).start()
+                        remote(part.at[c, ref], exr.at[c, ref], es.at[lax.rem(u, NC)], er.at[lax.rem(u, NC), m], partner).start()
 
             return carry
 
@@ -286,7 +285,7 @@
         def _():
             for m in range(NY):
                 remote(
-                    part.at[c, (1 - core) * NY + m], exr.at[c, m], es.at[u], er.at[u, m], partner
+                    part.at[c, (1 - core) * NY + m], exr.at[c, m], es.at[lax.rem(u, NC)], er.at[lax.rem(u, NC), m], partner
                 ).start()
 
         @pl.when(u == NC - 1)
@@ -309,17 +308,17 @@
 
     def chip_sum(u):
         c = lax.rem(u, NC)
-        drain(tok.at[u, 0:6], zs.at[u])
-        drain(recv.at[u, 0:NZ * (NX - 1)], xs.at[u])
+        drain(tok.at[u, 0:6], zs.at[lax.rem(u, NC)])
+        drain(recv.at[u, 0:NZ * (NX - 1)], xs.at[lax.rem(u, NC)])
 
         @pl.when(u < NC)
         def _():
             for i in (2, 3, 1):
                 to = lax.rem(y + i, NY)
                 mine = core * NY + to
-                drain(exr.at[c, to], er.at[u, to])
+                drain(exr.at[c, to], er.at[lax.rem(u, NC), to])
                 part[c, mine] = (part[c, mine].astype(F32) + exr[c, to].astype(F32)).astype(BF16)
-                remote(part.at[c, mine], yr.at[c, i - 1, 0], ys.at[u], yrs.at[u], at_y(to)).start()
+                remote(part.at[c, mine], yr.at[c, i - 1, 0], ys.at[lax.rem(u, NC)], yrs.at[lax.rem(u, NC)], at_y(to)).start()
 
         @pl.when(u >= NC)
         def _():
@@ -330,39 +329,39 @@
             for i in (2, 3, 1):
                 to = lax.rem(y + i, NY)
                 ref = pl.ds(2 * to, 2)
-                drain(exr.at[c, ref], er.at[u, to])
+                drain(exr.at[c, ref], er.at[lax.rem(u, NC), to])
                 for h in range(2):
                     m = 2 * to + h
                     part[c, m] = (part[c, m].astype(F32) + exr[c, m].astype(F32)).astype(BF16)
-                remote(part.at[c, ref], yr.at[c, i - 1], ys.at[u], yrs.at[u], at_y(to)).start()
-
-    def finish(u):
+                remote(part.at[c, ref], yr.at[c, i - 1], ys.at[lax.rem(u, NC)], yrs.at[lax.rem(u, NC)], at_y(to)).start()
+
+    def finish_down(u):
+        c = u
+        drain(exr.at[c, y], er.at[lax.rem(u, NC), y])
+        drain(part.at[c, 0:NY - 1], yrs.at[lax.rem(u, NC)])
+        total = part[c, core * NY + y].astype(F32) + exr[c, y].astype(F32)
+        for i in range(NY - 1):
+            total = total + yr[c, i, 0].astype(F32)
+        for i in range(DC // 128):
+            down_ref[:, pl.ds(pl.multiple_of(c * DC + i * 128, 128), 128)] = (
+                total[i * BLK:(i + 1) * BLK]
+            )
+        cols = pl.ds(pl.multiple_of(c * DC, DC), DC)
+        pltpu.make_async_copy(down_ref.at[:, cols], down_hbm.at[:, cols], od.at[0]).start()
+        pl.semaphore_signal(cx.at[c], inc=1, device_id=partner, device_id_type=MESH)
+        for i in range(1, NY):
+            pl.semaphore_signal(cy.at[c], inc=1, device_id=at_y(y + i), device_id_type=MESH)
+        drain(part.at[c, 0:NY], es.at[lax.rem(u, NC)])
+        drain(part.at[c, 0:NY - 1], ys.at[lax.rem(u, NC)])
+
+    def finish_up(u):
         c = lax.rem(u, NC)
         own = core == lax.rem(c, 2)
 
-        @pl.when(u < NC)
-        def _():
-            drain(exr.at[c, y], er.at[u, y])
-            drain(part.at[c, 0:NY - 1], yrs.at[u])
-            total = part[c, core * NY + y].astype(F32) + exr[c, y].astype(F32)
-            for i in range(NY - 1):
-                total = total + yr[c, i, 0].astype(F32)
-            for i in range(DC // 128):
-                down_ref[:, pl.ds(pl.multiple_of(c * DC + i * 128, 128), 128)] = (
-                    total[i * BLK:(i + 1) * BLK]
-                )
-            cols = pl.ds(pl.multiple_of(c * DC, DC), DC)
-            pltpu.make_async_copy(down_ref.at[:, cols], down_hbm.at[:, cols], od.at[u]).start()
-            pl.semaphore_signal(cx.at[c], inc=1, device_id=partner, device_id_type=MESH)
-            for i in range(1, NY):
-                pl.semaphore_signal(cy.at[c], inc=1, device_id=at_y(y + i), device_id_type=MESH)
-            drain(part.at[c, 0:NY], es.at[u])
-            drain(part.at[c, 0:NY - 1], ys.at[u])
-
-        @pl.when((u >= NC) & own)
-        def _():
-            drain(exr.at[c, pl.ds(2 * y, 2)], er.at[u, y])
-            drain(yr.at[c], yrs.at[u])
+        @pl.when(own)
+        def _():
+            drain(exr.at[c, pl.ds(2 * y, 2)], er.at[lax.rem(u, NC), y])
+            drain(yr.at[c], yrs.at[lax.rem(u, NC)])
             for h in range(2):
                 total = part[c, 2 * y + h].astype(F32) + exr[c, 2 * y + h].astype(F32)
                 for i in range(NY - 1):
@@ -371,12 +370,12 @@
                     pl.ds(pl.multiple_of(lax.div(c, 2) * 128, 128), 128), h * HALF:(h + 1) * HALF
                 ] = total.T.astype(BF16)
             out = pl.ds(pl.multiple_of(lax.div(c, 2) * 128, 128), 128)
-            pltpu.make_async_copy(upo_ref.at[out], up_out.at[out], od.at[u]).start()
-            drain(yr.at[c], ys.at[u])
-
-        @pl.when((u >= NC) & (core != lax.rem(c, 2)))
-        def _():
-            drain(part.at[c], es.at[u])
+            pltpu.make_async_copy(upo_ref.at[out], up_out.at[out], od.at[1]).start()
+            drain(yr.at[c], ys.at[lax.rem(u, NC)])
+
+        @pl.when(jnp.logical_not(own))
+        def _():
+            drain(part.at[c], es.at[lax.rem(u, NC)])
 
     def grads_over_z():
         drain(sg1r.at[0:NX - 1], misc.at[3])
@@ -410,36 +409,44 @@
         drain(sg2.at[0:NZ - 1], misc.at[4])
 
     def body(k, carry):
-        @pl.when((k + AHEAD < UNITS) & (k + AHEAD > 0))
+        on(k, 0, relay1)
+        on(k, 4, chip_sum)
+        on(k, 1, relay3)
+
+        @pl.when(k + AHEAD < UNITS)
         def _():
             send_own(k + AHEAD)
 
-        on(k, 1, relay1)
-        on(k, 2, relay2)
-        on(k, 3, relay3)
-        on(k, 1, pick1)
-        on(k, 2, pick2)
-        on(k, 3, pick3)
-        on(k, 4, pick4)
-        on(k, 5, compute)
-        on(k, 7, chip_sum)
-        on(k, 9, finish)
+        on(k, 0, pick1)
+        on(k, 1, pick3)
+        on(k, 2, pick4)
+        on(k, 3, compute)
+
+        @pl.when((k >= 6) & (k < NC + 6))
+        def _():
+            finish_down(k - 6)
+
+        @pl.when(k == NC + 3)
+        def _():
+            grads_over_z()
 
         @pl.when(k == NC + 5)
         def _():
-            grads_over_z()
-
-        @pl.when(k == NC + 6)
-        def _():
             grads_out()
 
+        on(k, 0, relay2)
+        on(k, 0, pick2)
         return carry
 
-    lax.fori_loop(0, UNITS + 9, body, 0)
-    for c in range(NC):
-        drain(down_ref.at[:, c * DC:(c + 1) * DC], od.at[c])
-    for q in range(NC // 2):
-        drain(upo_ref.at[q * 128:(q + 1) * 128], od.at[NC + 2 * q + core])
+    lax.fori_loop(0, UNITS + 4, body, 0)
+
+    def last(u, carry):
+        finish_up(u)
+        return carry
+
+    lax.fori_loop(NC, UNITS, last, 0)
+    drain(down_ref, od.at[0])
+    drain(upo_ref, od.at[1])
 
 
 def per_device(tokens, out_grad, probs, routes, saved_gate, saved_up, down_weight):
@@ -479,16 +486,16 @@
             pltpu.VMEM((NZ, 8, TOK), F32),
             pltpu.VMEM((BLK, D), F32),
             pltpu.VMEM((D // 8, FF), BF16),
-            dma((UNITS + 3,)),
-            dma((UNITS,)),
-            dma((UNITS,)),
-            dma((UNITS, NZ)),
-            dma((UNITS,)),
-            dma((UNITS,)),
-            dma((UNITS,)),
-            dma((UNITS, NY)),
-            dma((UNITS,)),
-            dma((UNITS,)),
+            dma((NC + 4,)),
+            dma((2,)),
+            dma((NC,)),
+            dma((NC, NZ)),
+            dma((NC,)),
+            dma((NC,)),
+            dma((NC,)),
+            dma((NC, NY)),
+            dma((NC,)),
+            dma((NC,)),
             dma((8,)),
             pltpu.SemaphoreType.REGULAR((NC,)),
             pltpu.SemaphoreType.REGULAR((NC,)),

time: 188 us -> 178 us (0.947)
  Pallas kernels: 183 us -> 173 us
    pallas_call x1, Pallas kernels: 183 us -> 173 us  [per_device(): pl.pallas_call(kernel, out_shape=(jax.ShapeDtypeStruct((BLK, D), F32), ja...]
where the time goes in v3:
time: 178 us; the launch traced here: 177 us
  Pallas kernels  173 us (97%)
  local copies, waits for them, and re-layouts  4.2 us (2%)
    pallas_call x1, Pallas kernels, per_device(): pl.pallas_call(kernel, out_shape=(jax.ShapeDtypeStruct((BLK, D), F32), ja...  173 us
    unnamed x7, local copies, waits for them, and re-layouts  4.2 us

profile of v3, /device:TPU:1, one launch (start us, length us, event | category | flops | bytes accessed | tf_op | source)
XLA Modules:
  0.0 177.4 jit_solution(14161301396558429045)
XLA Ops:
  0.6 172.5 %expert_grads.1 = (f32[96,4096]{1,0:T(8,128)}, bf16[512,768]{1,0:T(8,128)(2,1)}, f32[8,128]{1,0:T(8,128)}) custom-call(bf16[128,4096]{1,0:T(8,128)(2,1)} %x_hbm.1, bf16[128,4096]{1,0:T(8,128)(2,1)} %dy_hbm.1, bf16[8,128]{1,0:T(8,128)(2,1)} %bitcast.11, s32[8,128]{1,0:T(8,128)} %bitcast.9, bf16[512,768]{1,0:T(8,128)(2,1)} %gate_hbm.1, ...), custom_call_target="tpu_custom_call" | custom-call | tf_op jit(solution)/shard_map/expert_grads/pallas_call | solution.py:456
  173.1 0.0 copy-start
  173.2 0.0 copy-start.1
  173.2 2.7 %copy.13 = f32[1,96,4096]{2,1,0:T(8,128)} copy(f32[1,96,4096]{2,1,0:T(8,128)} %bitcast.7) | data formatting | bytes 3145728
  175.9 0.0 copy-done
  175.9 0.9 copy.14
  176.8 0.0 copy-done.1
  176.8 0.6 copy.15
Async XLA Ops:
  173.1 2.7 %copy-start = (bf16[512,768]{1,0:T(8,128)(2,1)S(1)}, bf16[512,768]{1,0:T(8,128)(2,1)}, u32[]{:S(2)}) copy-start(bf16[512,768]{1,0:T(8,128)(2,1)} %get-tuple-element.7) | copy-start | bytes 2359300
  173.2 3.6 %copy-start.1 = (f32[8,128]{1,0:T(8,128)S(1)}, f32[8,128]{1,0:T(8,128)}, u32[]{:S(2)}) copy-start(f32[8,128]{1,0:T(8,128)} %get-tuple-element.8) | copy-start | bytes 12292

commit v4 on v3

--- a/solution.py
+++ b/solution.py
@@ -447,6 +447,12 @@
     lax.fori_loop(NC, UNITS, last, 0)
     drain(down_ref, od.at[0])
     drain(upo_ref, od.at[1])
+
+
+def hand_over(down_ref, up_ref, pg_ref, down_out, up_out, pg_out):
+    down_out[...] = down_ref[...]
+    up_out[...] = up_ref[...]
+    pg_out[...] = pg_ref[...]
 
 
 def per_device(tokens, out_grad, probs, routes, saved_gate, saved_up, down_weight):
@@ -508,6 +514,13 @@
         tokens, out_grad, probs.T, routes.T, saved_gate, saved_up,
         down_weight.reshape(down_weight.shape[1:]),
     )
+    down, up, pg = pl.pallas_call(
+        hand_over,
+        out_shape=tuple(jax.ShapeDtypeStruct(a.shape, a.dtype) for a in (down, up, pg)),
+        in_specs=[vmem, vmem, vmem],
+        out_specs=(vmem, vmem, vmem),
+        name="hand_over",
+    )(down, up, pg)
     return down[None], up[None], pg.T
 
 

time: 178 us -> 176 us (0.989)
  local copies, waits for them, and re-layouts: 4.2 us -> 0 us
  Pallas kernels: 173 us -> 176 us
    unnamed x7 -> x0, local copies, waits for them, and re-layouts: 4.2 us -> none
    pallas_call x0 -> x1, Pallas kernels: none -> 3.11 us  [per_device(): pl.pallas_call(hand_over, out_shape=tuple((jax.ShapeDtypeStruct(a.shape,...]
where the time goes in v4:
time: 176 us
  Pallas kernels  176 us (100%)
    pallas_call x1, Pallas kernels, per_device(): pl.pallas_call(kernel, out_shape=(jax.ShapeDtypeStruct((BLK, D), F32), ja...  173 us

profile of v4, /device:TPU:1, one launch (start us, length us, event | category | flops | bytes accessed | tf_op | source)
XLA Modules:
  0.0 176.3 jit_solution(17978202091682736222)
XLA Ops:
  0.6 172.5 %expert_grads.1 = (f32[96,4096]{1,0:T(8,128)}, bf16[512,768]{1,0:T(8,128)(2,1)}, f32[8,128]{1,0:T(8,128)}) custom-call(bf16[128,4096]{1,0:T(8,128)(2,1)} %x_hbm.1, bf16[128,4096]{1,0:T(8,128)(2,1)} %dy_hbm.1, bf16[8,128]{1,0:T(8,128)(2,1)} %bitcast.8, s32[8,128]{1,0:T(8,128)} %bitcast.7, bf16[512,768]{1,0:T(8,128)(2,1)} %gate_hbm.1, ...), custom_call_target="tpu_custom_call" | custom-call | tf_op jit(solution)/shard_map/expert_grads/pallas_call | solution.py:462
  173.2 3.1 %hand_over.1 = (f32[96,4096]{1,0:T(8,128)}, bf16[512,768]{1,0:T(8,128)(2,1)}, f32[8,128]{1,0:T(8,128)}) custom-call(f32[96,4096]{1,0:T(8,128)} %get-tuple-element.9.down_ref, bf16[512,768]{1,0:T(8,128)(2,1)} %get-tuple-element.10.up_ref, f32[8,128]{1,0:T(8,128)} %get-tuple-element.11.pg_ref), custom_call_target="tpu_custom_call" | custom-call | tf_op jit(solution)/shard_map/hand_over/pallas_call | solution.py:517
